TPU v7x, 32 devices: a whole 2x2x4 slice. The times are simulated.
32 devices in a mesh: dp: 8 (over z, y), tensor: 4 (over x, core).
Axes of the slice: x: 2, y: 2, z: 4, core: 2. Of those that a mesh axis runs over, the one named last changes fastest.
Arguments:
- inputs: bfloat16 [1024, 3200], P('dp'), may hold values from -6 to 6
- norm_gain: float32 [3200], replicated, may hold values from 0.25 to 1.75
- fc1_weight: bfloat16 [3200, 8192], P(None, 'tensor'), may hold values from -0.109375 to 0.109375
- fc1_bias: float32 [8192], P('tensor'), may hold values from -4 to 4
- grad_act: bfloat16 [1024, 8192], P('dp', 'tensor'), may hold values from -6 to 6
- grad_res: bfloat16 [1024, 3200], P(('dp', 'tensor')), may hold values from -6 to 6
Outputs:
- grad_inputs: bfloat16 [1024, 3200], P(('dp', 'tensor'))
- grad_weight: float32 [3200, 8192], P('dp', 'tensor')
- grad_bias: float32 [8192], P('tensor')
- grad_gain: float32 [3200], replicated
All inputs are finite; a program needn't handle non-finite values.
Results may differ from a plain program's by a relative error of at most 0.008.
Values may be sent and summed in bfloat16 or wider, within the bound.
No kernel may reach another device: no remote copies, remote signals or barrier semaphores. Data moves between devices by JAX's collectives and lax.ppermute only.
A program may use at most 192 MiB of HBM per device.

v0:
```python
import jax
import jax.numpy as jnp
from jax import lax
from jax.sharding import PartitionSpec as P

epsilon = 1e-06


def on_device(inputs, norm_gain, fc1_weight, fc1_bias, grad_act, grad_res):
    values = inputs.astype(jnp.float32)
    inverse = lax.rsqrt(jnp.mean(values * values, axis=-1, keepdims=True) + epsilon)
    normalized = values * inverse
    normed = (normalized * norm_gain).astype(jnp.bfloat16)
    preact = jnp.dot(normed, fc1_weight, preferred_element_type=jnp.float32) + fc1_bias
    derivative = (
        0.5 * (1.0 + lax.erf(preact * 0.7071067811865476))
        + preact * jnp.exp(-0.5 * preact * preact) * 0.3989422804014327
    )
    grad_pre = (grad_act.astype(jnp.float32) * derivative).astype(jnp.bfloat16)
    bias_part = jnp.sum(grad_pre.astype(jnp.float32), axis=0)
    back_term = lax.dot_general(
        grad_pre, fc1_weight, (((1,), (1,)), ((), ())), preferred_element_type=jnp.float32
    )
    dnormed = lax.psum_scatter(
        back_term.astype(jnp.bfloat16), "tensor", scatter_dimension=0, tiled=True
    ).astype(jnp.float32)
    dp_size = lax.axis_size("dp")
    width_all = normed.shape[1]
    cols_local = grad_pre.shape[1]
    owner_rows = width_all // dp_size
    weight_term = lax.dot_general(
        normed, grad_pre, (((0,), (0,)), ((), ())), preferred_element_type=jnp.float32
    )
    flat_term = weight_term.reshape(dp_size, owner_rows * cols_local)
    owned = lax.psum_scatter(flat_term, "dp", scatter_dimension=0, tiled=True)
    grad_weight = owned.reshape(owner_rows, cols_local)
    tensor_size = lax.axis_size("tensor")
    position = lax.axis_index("tensor")
    row_count = inputs.shape[0] // tensor_size
    row_start = position * row_count
    normalized_rows = lax.dynamic_slice_in_dim(normalized, row_start, row_count, 0)
    inverse_rows = lax.dynamic_slice_in_dim(inverse, row_start, row_count, 0)
    gain_part = jnp.sum(dnormed * normalized_rows, axis=0)
    grad_hat = dnormed * norm_gain
    projection = jnp.mean(grad_hat * normalized_rows, axis=-1, keepdims=True)
    grad_inputs = (
        grad_res.astype(jnp.float32) + inverse_rows * (grad_hat - normalized_rows * projection)
    ).astype(jnp.bfloat16)
    grad_gain = lax.psum(gain_part, ("dp", "tensor"))
    grad_bias = lax.psum(bias_part, "dp")
    return (grad_inputs, grad_weight, grad_bias, grad_gain)


def solution(mesh):
    in_specs = (
        P("dp", None),
        P(),
        P(None, "tensor"),
        P("tensor"),
        P("dp", "tensor"),
        P(("dp", "tensor"), None),
    )
    out_specs = (P(("dp", "tensor"), None), P("dp", "tensor"), P("tensor"), P())
    return jax.shard_map(
        on_device, mesh=mesh, in_specs=in_specs, out_specs=out_specs, check_vma=False
    )
```

profile of v0, /device:TPU:0, one launch (start us, length us, event | category | flops | bytes accessed | tf_op | source)
XLA Modules:
  0.0 878.5 jit_solution(11047269485158148202)
XLA Ops:
  8.0 0.0 reduce-scatter.2.cloned.1.call-start
  8.0 0.0 slice-start
  8.1 1.5 fusion
  9.6 0.0 slice-start.1
  9.6 0.0 slice-start.2
  9.6 0.0 slice-start.3
  9.6 7.8 convert_reduce_fusion
  17.4 0.0 slice-done
  17.4 0.0 slice-done.1
  17.4 0.0 slice-done.2
  17.4 0.0 slice-done.3
  17.5 0.0 copy-start
  17.5 0.0 copy-start.2
  17.5 5.2 convolution_convert_fusion
  22.7 0.0 reduce-scatter.2.cloned.1.call-update
  22.7 0.2 all-reduce.3.cloned.1.call-start
  22.9 0.0 copy-done
  23.0 0.0 copy-done.2
  23.0 11.0 %fusion.14 = f32[3200,2048]{1,0:T(8,128)} fusion(bf16[128,2048]{1,0:T(8,128)(2,1)S(1)} %get-tuple-element.7, f32[3200]{0:T(1024)S(1)} %copy-done.2, bf16[128,3200]{1,0:T(8,128)(2,1)S(1)} %copy-done, f32[128]{0:T(128)S(1)} %add_rsqrt_fusion), kind=kOutput, calls=%fused_computation.24 | convolution fusion | flops 1679360000 | bytes 27571200 | tf_op jit(solution)/shard_map/dot_general | solution.py:31
  33.9 23.7 %reshape.43 = f32[8,819200]{1,0:T(8,128)} reshape(f32[3200,2048]{1,0:T(8,128)} %fusion.14) | data formatting | bytes 52428800 | tf_op jit(solution)/shard_map/reshape | solution.py:34
  57.6 0.0 copy-start.3
  57.6 0.0 all-reduce.3.cloned.1.call-update
  57.6 0.0 copy-start.1
  57.6 0.1 dynamic-slice.3
  57.7 0.5 copy-done.3
  58.3 0.7 dynamic-slice.4
  58.9 25.5 %psum.14 = f32[2048]{0:T(1024)} all-reduce(f32[2048]{0:T(1024)S(1)} %get-tuple-element.6), channel_id=1, replica_groups=mesh['dp'=8,'tensor'=4] {'dp'}, use_global_device_ids=true, to_apply=%region_5.0 | all-reduce | flops 2048 | bytes 16384 | tf_op jit(solution)/shard_map/psum | solution.py:50
  84.4 0.2 convert_multiply_fusion
  84.6 0.0 reduce-scatter.2.cloned.1.call-done
  84.7 1.2 fusion.13
  85.8 41.9 %psum.15 = f32[3200]{0:T(1024)} all-reduce(f32[3200]{0:T(1024)S(1)} %get-tuple-element.4), channel_id=1, replica_groups=mesh['dp'=8,'tensor'=4] {'dp','tensor'}, use_global_device_ids=true, to_apply=%region_7.0 | all-reduce | flops 3200 | bytes 25600 | tf_op jit(solution)/shard_map/psum | solution.py:49
  127.7 0.0 copy-done.1
  127.7 1.8 fusion.12
  129.5 702.9 %all-reduce.3.cloned.1.call-done = f32[8,819200]{1,0:T(8,128)} async-done(((f32[8,819200]{1,0:T(8,128)}), f32[8,819200]{1,0:T(8,128)}) %all-reduce.3.cloned.1.call-update) | async-done | bytes 26214416
  832.4 36.7 %dynamic-slice_reduce_fusion = f32[819200]{0:T(1024)S(1)} fusion(f32[8,819200]{1,0:T(8,128)} %all-reduce.3.cloned.1.call-done, u32[]{:T(128)} %bitcast), kind=kLoop, calls=%fused_computation.1 | loop fusion | bytes 6553604
  869.1 1.9 reshape.44
  (3 shorter events, 0.0 us)
Async XLA Ops:
  8.0 76.6 %reduce-scatter.2.cloned.1.call-start = ((), (), s32[]{:S(2)}) async-start(), calls=%async_computation.1 | async-start | bytes 1024000 | tf_op jit(solution)/shard_map/reduce_scatter | solution.py:24
  8.0 9.4 %slice-start = ((s8[13107200]{0:T(1024)(128)(4,1)}), s8[4194304]{0:T(1024)(128)(4,1)S(1)}, s32[]{:S(2)}) async-start(s8[13107200]{0:T(1024)(128)(4,1)} %bitcast.5), calls=%async_computation.3 | async-start | bytes 8388608
  9.6 7.8 slice-start.1
  9.6 7.8 slice-start.2
  9.6 7.8 slice-start.3
  17.5 5.5 copy-start
  17.5 5.5 copy-start.2
  22.7 809.7 %all-reduce.3.cloned.1.call-start = ((), (), s32[]{:S(2)}) async-start(), calls=%async_computation.2 | async-start | bytes 52428800
  57.6 0.7 copy-start.3
  57.6 70.1 %copy-start.1 = (bf16[32,3200]{1,0:T(8,128)(2,1)S(1)}, bf16[32,3200]{1,0:T(8,128)(2,1)}, u32[]{:S(2)}) copy-start(bf16[32,3200]{1,0:T(8,128)(2,1)} %param.11) | copy-start | bytes 614404
Sparse Core Ops, SparseCore 0:
  22.8 26.1 reduce-scatter.1
Sparse Core Ops, SparseCore 1:
  57.7 774.6 all-reduce.2
where the time goes:
time: 879 us; the launch traced here: 878 us
  waiting for transfers between devices  703 us (80%)
  blocking collectives  67.4 us (8%)
  local copies, waits for them, and re-layouts  63.6 us (7%)
  matrix products  23.9 us (3%)
  between operations  15.6 us (2%)
    unnamed x3, waiting for transfers between devices  703 us
    psum x1, blocking collectives, on_device(): grad_gain = lax.psum(gain_part, ('dp', 'tensor'))  41.9 us
    unnamed x18, local copies, waits for them, and re-layouts  37.9 us
    psum x1, blocking collectives, on_device(): grad_bias = lax.psum(bias_part, 'dp')  25.5 us
    reshape x1, local copies, waits for them, and re-layouts, on_device(): flat_term = weight_term.reshape(dp_size, owner_rows * cols_local)  23.7 us
  transfers between devices with their start and end apart: 2, of which 1 were waited for; matrix products, arithmetic and copies ran while one was open for 4% of the time, Pallas kernels for 0%

commit v1 on v0

v1 whole, which is shorter than its diff:
```python
import jax
import jax.numpy as jnp
from jax import lax
from jax.sharding import PartitionSpec as P

epsilon = 1e-06


def on_device(inputs, norm_gain, fc1_weight, fc1_bias, grad_act, grad_res):
    dp_size = lax.axis_size("dp")
    tensor_size = lax.axis_size("tensor")
    tokens, width = inputs.shape
    owner_rows = width // dp_size
    values = inputs.astype(jnp.float32)
    inverse = lax.rsqrt(jnp.mean(values * values, axis=-1, keepdims=True) + epsilon)
    normalized = values * inverse
    normed = (normalized * norm_gain).astype(jnp.bfloat16)
    blocks = normed.reshape(tokens, dp_size, owner_rows).transpose(1, 0, 2)
    owned_cols = lax.all_to_all(blocks, "dp", 0, 0, tiled=True).reshape(dp_size * tokens, owner_rows)
    preact = jnp.dot(normed, fc1_weight, preferred_element_type=jnp.float32) + fc1_bias
    derivative = (
        0.5 * (1.0 + lax.erf(preact * 0.7071067811865476))
        + preact * jnp.exp(-0.5 * preact * preact) * 0.3989422804014327
    )
    grad_pre = (grad_act.astype(jnp.float32) * derivative).astype(jnp.bfloat16)
    grad_pre_all = lax.all_gather(grad_pre, "dp", axis=0, tiled=True)
    back_term = lax.dot_general(
        grad_pre, fc1_weight, (((1,), (1,)), ((), ())), preferred_element_type=jnp.float32
    )
    dnormed = lax.psum_scatter(
        back_term.astype(jnp.bfloat16), "tensor", scatter_dimension=0, tiled=True
    ).astype(jnp.float32)
    grad_weight = lax.dot_general(
        owned_cols, grad_pre_all, (((0,), (0,)), ((), ())), preferred_element_type=jnp.float32
    )
    grad_bias = jnp.sum(grad_pre_all.astype(jnp.float32), axis=0)
    row_count = tokens // tensor_size
    row_start = lax.axis_index("tensor") * row_count
    normalized_rows = lax.dynamic_slice_in_dim(normalized, row_start, row_count, 0)
    inverse_rows = lax.dynamic_slice_in_dim(inverse, row_start, row_count, 0)
    gain_part = jnp.sum(dnormed * normalized_rows, axis=0)
    grad_hat = dnormed * norm_gain
    projection = jnp.mean(grad_hat * normalized_rows, axis=-1, keepdims=True)
    grad_inputs = (
        grad_res.astype(jnp.float32) + inverse_rows * (grad_hat - normalized_rows * projection)
    ).astype(jnp.bfloat16)
    grad_gain = lax.psum(gain_part, ("dp", "tensor"))
    return (grad_inputs, grad_weight, grad_bias, grad_gain)


def solution(mesh):
    in_specs = (
        P("dp", None),
        P(),
        P(None, "tensor"),
        P("tensor"),
        P("dp", "tensor"),
        P(("dp", "tensor"), None),
    )
    out_specs = (P(("dp", "tensor"), None), P("dp", "tensor"), P("tensor"), P())
    return jax.shard_map(
        on_device, mesh=mesh, in_specs=in_specs, out_specs=out_specs, check_vma=False
    )
```

time: 879 us -> 138 us (0.16)
  waiting for transfers between devices: 703 us -> 38.2 us
  local copies, waits for them, and re-layouts: 63.6 us -> 1.39 us
  blocking collectives: 67.4 us -> 41.7 us
    unnamed x3 -> x2, waiting for transfers between devices: 703 us -> 0.54 us
    unnamed x18 -> x6, local copies, waits for them, and re-layouts: 37.9 us -> 0.01 us
    reshape x2 -> x0, local copies, waits for them, and re-layouts: 25.6 us -> none  [the longest x1 23.7 us: on_device(): flat_term = weight_term.reshape(dp_size, owner_rows * cols_local)]
    psum x1 -> x0, blocking collectives: 25.5 us -> none  [on_device(): grad_bias = lax.psum(bias_part, 'dp')]
    all_gather x0 -> x1, waiting for transfers between devices: none -> 20.6 us  [on_device(): grad_pre_all = lax.all_gather(grad_pre, 'dp', axis=0, tiled=True)]
    reduce_scatter x1, waiting for transfers between devices: 0.02 us -> 17 us  [on_device(): lax.psum_scatter(back_term.astype(jnp.bfloat16), 'tensor', scatter_dimens...]
  transfers between devices with their start and end apart: 2 -> 3, of which waited for: 1 -> 2; matrix products, arithmetic and copies ran while one was open for 4% -> 6% of each run, Pallas kernels for 0% -> 0%
where the time goes in v1:
time: 138 us; the launch traced here: 137 us
  blocking collectives  41.7 us (30%)
  waiting for transfers between devices  38.2 us (28%)
  matrix products  23.8 us (17%)
  between operations  15.5 us (11%)
  other arithmetic  9.2 us (7%)
  starting transfers between devices  7.39 us (5%)
  local copies, waits for them, and re-layouts  1.39 us (1%)
    psum x1, blocking collectives, on_device(): grad_gain = lax.psum(gain_part, ('dp', 'tensor'))  41.7 us
    all_gather x1, waiting for transfers between devices, on_device(): grad_pre_all = lax.all_gather(grad_pre, 'dp', axis=0, tiled=True)  20.6 us
    reduce_scatter x1, waiting for transfers between devices, on_device(): lax.psum_scatter(back_term.astype(jnp.bfloat16), 'tensor', scatter_dimens...  17 us
    dot_general x1, matrix products, on_device(): lax.dot_general(grad_pre, fc1_weight, (((1,), (1,)), ((), ())), preferred...  10 us
    dot_general x1, matrix products, on_device(): jnp.dot(normed, fc1_weight, preferred_element_type=jnp.float32) + fc1_bias  8 us
    all_to_all x1, starting transfers between devices, on_device(): lax.all_to_all(blocks, 'dp', 0, 0, tiled=True)  7.31 us
    dot_general x1, matrix products, on_device(): lax.dot_general(owned_cols, grad_pre_all, (((0,), (0,)), ((), ())), prefe...  5.75 us
    reduce_sum x1, other arithmetic, on_device(): grad_bias = jnp.sum(grad_pre_all.astype(jnp.float32), axis=0)  3.42 us
  transfers between devices with their start and end apart: 3, of which 2 were waited for; matrix products, arithmetic and copies ran while one was open for 6% of the time, Pallas kernels for 0%

profile of v1, /device:TPU:0, one launch (start us, length us, event | category | flops | bytes accessed | tf_op | source)
XLA Modules:
  0.0 137.2 jit_solution(2387657877034527978)
XLA Ops:
  8.0 0.0 copy-start
  8.0 0.0 reduce-scatter.2.cloned.1.call-start
  8.1 1.4 %fusion = f32[128]{0:T(128)S(1)} fusion(bf16[128,3200]{1,0:T(8,128)(2,1)} %param.6), kind=kLoop, calls=%fused_computation.5 | loop fusion | flops 1228672 | bytes 819712 | tf_op jit(solution)/shard_map/reduce_sum | solution.py:15
  9.5 1.4 %convert_multiply_fusion = (f32[128,3200]{1,0:T(8,128)S(1)}, bf16[128,3200]{1,0:T(8,128)(2,1)S(1)}) fusion(bf16[128,3200]{1,0:T(8,128)(2,1)} %param.6, f32[128]{0:T(128)S(1)} %add_rsqrt_fusion, f32[3200]{0:T(1024)} %param.7), kind=kLoop, calls=%fused_computation.3 | loop fusion | flops 1638400 | bytes 3290112 | tf_op jit(solution)/shard_map/mul | solution.py:16
  10.9 0.0 copy-done
  10.9 8.0 %fusion.6 = (bf16[128,2048]{1,0:T(8,128)(2,1)}, f32[128,2048]{1,0:T(8,128)S(1)}) fusion(bf16[128,2048]{1,0:T(8,128)(2,1)S(1)} %copy-done, f32[2048]{0:T(1024)} %param.9, bf16[128,3200]{1,0:T(8,128)(2,1)S(1)} %get-tuple-element.7, bf16[3200,2048]{1,0:T(8,128)(2,1)} %param.8), kind=kOutput, calls=%fused_computation.13 | convolution fusion | flops 1680867328 | bytes 16031744 | tf_op jit(solution)/shard_map/dot_general | solution.py:20
  18.9 10.0 %convolution_convert_fusion = bf16[128,3200]{1,0:T(8,128)(2,1)} fusion(bf16[3200,2048]{1,0:T(8,128)(2,1)} %param.8, f32[128,2048]{1,0:T(8,128)S(1)} %get-tuple-element.9, bf16[128,2048]{1,0:T(8,128)(2,1)S(1)} %copy-done), kind=kOutput, calls=%fused_computation.1 | convolution fusion | flops 1681014784 | bytes 15499264 | tf_op jit(solution)/shard_map/dot_general | solution.py:27
  28.9 0.0 copy-start.2
  28.9 0.0 copy-start.1
  28.9 0.0 reduce-scatter.2.cloned.1.call-update
  29.0 0.0 all-gather.2.cloned.1.call-start
  29.0 0.5 all-gather.2.cloned.1.call-update
  29.5 1.3 copy.10
  30.8 7.3 %all-to-all-start = ((bf16[8,128,400]{1,2,0:T(8,128)(2,1)}), bf16[8,128,400]{1,2,0:T(8,128)(2,1)S(1)}, u32[]{:S(2)}, u32[]{:S(2)}) async-start(bf16[8,128,400]{1,2,0:T(8,128)(2,1)} %bitcast.1), calls=%async_computation.1 | async-start | bytes 1638400 | tf_op jit(solution)/shard_map/all_to_all | solution.py:19
  38.2 0.1 dynamic-slice.3
  38.2 17.0 %reduce-scatter.2.cloned.1.call-done = bf16[32,3200]{1,0:T(8,128)(2,1)} async-done(((bf16[128,3200]{1,0:T(8,128)(2,1)}), bf16[32,3200]{1,0:T(8,128)(2,1)}) %reduce-scatter.2.cloned.1.call-update) | async-done | bytes 204816 | tf_op jit(solution)/shard_map/reduce_scatter | solution.py:30
  55.3 0.0 copy-done.2
  55.3 1.1 fusion.23
  56.4 41.7 %psum.7 = f32[3200]{0:T(1024)} all-reduce(f32[3200]{0:T(1024)S(1)} %get-tuple-element.4), channel_id=1, replica_groups=mesh['dp'=8,'tensor'=4] {'dp','tensor'}, use_global_device_ids=true, to_apply=%region_5.0 | all-reduce | flops 3200 | bytes 25600 | tf_op jit(solution)/shard_map/psum | solution.py:47
  98.1 0.0 copy-done.1
  98.1 1.8 %fusion.22 = bf16[32,3200]{1,0:T(8,128)(2,1)} fusion(bf16[32,3200]{1,0:T(8,128)(2,1)} %reduce-scatter.2.cloned.1.call-done, bf16[32,3200]{1,0:T(8,128)(2,1)S(1)} %copy-done.1, f32[128,3200]{1,0:T(8,128)S(1)} %get-tuple-element.6, s32[]{:T(128)S(6)} %select_n.4, f32[32]{0:T(128)S(1)} %broadcast_multiply_fusion, f32[3200]{0:T(1024)S(1)} %copy-done.2, ...), kind=kLoop, calls=%fused_computation.30 | loop fusion | flops 819200 | bytes 1037060 | tf_op jit(solution)/shard_map/convert_element_type | solution.py:46
  99.9 20.6 %all-gather.2.cloned.1.call-done = bf16[1024,2048]{1,0:T(8,128)(2,1)} async-done(((bf16[128,2048]{1,0:T(8,128)(2,1)}), bf16[1024,2048]{1,0:T(8,128)(2,1)}) %all-gather.2.cloned.1.call-update) | async-done | bytes 4194320 | tf_op jit(solution)/shard_map/all_gather | solution.py:26
  120.5 3.4 %convert_reduce_fusion = f32[2048]{0:T(1024)} fusion(bf16[1024,2048]{1,0:T(8,128)(2,1)} %all-gather.2.cloned.1.call-done), kind=kLoop, calls=%fused_computation | loop fusion | flops 4192256 | bytes 4202496 | tf_op jit(solution)/shard_map/reduce_sum | solution.py:36
  124.0 0.0 all-to-all-done
  124.0 5.8 %fusion.9 = f32[400,2048]{1,0:T(8,128)} fusion(bf16[1024,2048]{1,0:T(8,128)(2,1)} %all-gather.2.cloned.1.call-done, bf16[8,128,400]{1,2,0:T(8,128)(2,1)S(1)} %all-to-all-done), kind=kOutput, calls=%fused_computation.15 | convolution fusion | flops 1677721600 | bytes 8290304 | tf_op jit(solution)/shard_map/dot_general | solution.py:33
  (2 shorter events, 0.0 us)
Async XLA Ops:
  8.0 2.9 %copy-start = (bf16[128,2048]{1,0:T(8,128)(2,1)S(1)}, bf16[128,2048]{1,0:T(8,128)(2,1)}, u32[]{:S(2)}) copy-start(bf16[128,2048]{1,0:T(8,128)(2,1)} %param.10) | copy-start | bytes 1572868
  8.0 47.3 %reduce-scatter.2.cloned.1.call-start = ((), (), s32[]{:S(2)}) async-start(), calls=%async_computation.2 | async-start | bytes 1024000 | tf_op jit(solution)/shard_map/reduce_scatter | solution.py:30
  28.9 26.3 %copy-start.2 = (f32[3200]{0:T(1024)S(1)}, f32[3200]{0:T(1024)}, u32[]{:S(2)}) copy-start(f32[3200]{0:T(1024)} %param.7) | copy-start | bytes 38404
  28.9 69.2 %copy-start.1 = (bf16[32,3200]{1,0:T(8,128)(2,1)S(1)}, bf16[32,3200]{1,0:T(8,128)(2,1)}, u32[]{:S(2)}) copy-start(bf16[32,3200]{1,0:T(8,128)(2,1)} %param.11) | copy-start | bytes 614404
  29.0 91.6 %all-gather.2.cloned.1.call-start = ((), (), s32[]{:S(2)}) async-start(), calls=%async_computation.3 | async-start | bytes 4718592 | tf_op jit(solution)/shard_map/all_gather | solution.py:26
  30.8 93.1 %all-to-all-start = ((bf16[8,128,400]{1,2,0:T(8,128)(2,1)}), bf16[8,128,400]{1,2,0:T(8,128)(2,1)S(1)}, u32[]{:S(2)}, u32[]{:S(2)}) async-start(bf16[8,128,400]{1,2,0:T(8,128)(2,1)} %bitcast.1), calls=%async_computation.1 | async-start | bytes 1638400 | tf_op jit(solution)/shard_map/all_to_all | solution.py:19
Sparse Core Ops, SparseCore 0:
  29.1 26.1 reduce-scatter.1
Sparse Core Ops, SparseCore 1:
  31.6 88.9 all-gather.1
